TPU v7x, 128 devices: a whole 4x4x4 slice. The times are simulated.
128 devices in a mesh: row: 8 (over x, core), col: 16 (over y, z).
Axes of the slice: x: 4, y: 4, z: 4, core: 2. Of those that a mesh axis runs over, the one named last changes fastest.
Arguments:
- a_matrix: float32 [32768, 24576], P('row', 'col'), may hold values from 0 to 1
- h_factor: float32 [256, 24576], P(None, 'col'), may hold values from 0 to 1
- w_factor: float32 [32768, 256], P('row'), may hold values from 0 to 0.0078125
- accept: int32 [32768, 2], P('row'), may hold values from 0 to 1
- shrink: int32 [32768, 2], P('row'), may hold values from 0 to 3
Outputs:
- w_new: float32 [32768, 256], P('row')
- grad_h: float32 [256, 24576], P('row', 'col')
- armijo: float32 [2, 2], replicated
All inputs are finite; a program needn't handle non-finite values.
Results may differ from a plain program's by a relative error of at most 0.00012.
Values sent between devices are 32-bit elements; how exact they have to be, the bound alone decides.
A program may use at most 192 MiB of HBM per device.

v0:
```python
import jax
import jax.numpy as jnp
from jax import lax
from jax.sharding import PartitionSpec as P


def copy_for_each(x, axis):
    peers = lax.axis_size(axis)
    return lax.all_to_all(jnp.broadcast_to(x[None], (peers, *x.shape)), axis, 0, 0, tiled=True)


def over_copies(x, axis):
    return copy_for_each(x, axis).sum(axis=0)


def cut_along(x, dim, peers):
    dims = x.shape
    parts = x.reshape(*dims[:dim], peers, dims[dim] // peers, *dims[dim + 1 :])
    return jnp.moveaxis(parts, dim, 0)


def sum_at_owner(x, axis, dim):
    peers = lax.axis_size(axis)
    parts = lax.all_to_all(cut_along(x, dim, peers), axis, 0, 0, tiled=True)
    return jnp.sum(parts, axis=0)


def run_trials(current, hh, ah, accept, shrink):
    highest = lax.Precision.HIGHEST
    step_size = hh.shape[0] / jnp.trace(hh)
    flags = accept.astype(jnp.float32)
    powers = shrink.astype(jnp.float32)
    results = []
    for trial in range(accept.shape[1]):
        gradient = jnp.dot(current, hh, precision=highest, preferred_element_type=jnp.float32) - ah
        factor = jnp.power(jnp.float32(0.5), powers[:, trial : trial + 1]) * step_size
        change = jnp.maximum(current - factor * gradient, 0.0) - current
        first = jnp.sum(gradient * change)
        second = jnp.sum(
            change * jnp.dot(change, hh, precision=highest, preferred_element_type=jnp.float32)
        )
        results.append(jnp.stack([first, second]))
        current = current + flags[:, trial : trial + 1] * change
    return (current, jnp.stack(results))


def per_device(a_matrix, h_factor, w_factor, accept, shrink):
    highest = lax.Precision.HIGHEST
    gram_part = jnp.dot(h_factor, h_factor.T, precision=highest, preferred_element_type=jnp.float32)
    ah_part = jnp.dot(a_matrix, h_factor.T, precision=highest, preferred_element_type=jnp.float32)
    hh, ah = lax.psum((gram_part, ah_part), "col")
    w_new, partial_stats = run_trials(w_factor, hh, ah, accept, shrink)
    armijo = over_copies(partial_stats, "row")
    residue = (
        jnp.dot(w_new, h_factor, precision=highest, preferred_element_type=jnp.float32) - a_matrix
    )
    columns = lax.slice_in_dim(
        w_new, 0, w_new.shape[1] // lax.axis_size("row") * lax.axis_size("row"), axis=1
    )
    grad_h = sum_at_owner(
        lax.dot_general(
            columns,
            residue,
            (((0,), (0,)), ((), ())),
            precision=highest,
            preferred_element_type=jnp.float32,
        ),
        "row",
        0,
    )
    return (w_new, grad_h, armijo)


def solution(mesh):
    in_specs = (P("row", "col"), P(None, "col"), P("row", None), P("row", None), P("row", None))
    out_specs = (P("row", None), P("row", "col"), P())
    return jax.shard_map(
        per_device, mesh=mesh, in_specs=in_specs, out_specs=out_specs, check_vma=False
    )
```

profile of v0, /device:TPU:1, one launch (start us, length us, event | category | flops | bytes accessed | tf_op | source)
XLA Modules:
  0.0 274.4 jit_solution(17738126336943551678)
XLA Ops:
  7.2 0.0 all-reduce.3.cloned.1.call-start
  7.2 1.4 copy-done
  8.6 2.2 fusion.14
  10.7 26.4 %fusion.15 = f32[4096,256]{0,1:T(8,128)} fusion(f32[4096,1536]{1,0:T(8,128)} %param.5, f32[256,1536]{1,0:T(8,128)S(1)} %copy-done), kind=kOutput, calls=%fused_computation.32 | convolution fusion | flops 19327352832 | bytes 30932992 | tf_op jit(solution)/shard_map/dot_general | solution.py:50
  37.2 0.0 all-reduce.3.cloned.1.call-update
  37.2 0.7 copy-done.5
  37.9 5.6 %copy.27 = f32[4096,256]{0,1:T(8,128)} copy(f32[4096,256]{1,0:T(8,128)} %param.7) | data formatting | bytes 8388608 | tf_op args[2]
  43.6 102.9 %all-reduce.3.cloned.1.call-done = (f32[4096,256]{0,1:T(8,128)}, f32[256,256]{1,0:T(8,128)}) async-done(((f32[4096,256]{0,1:T(8,128)}, f32[256,256]{1,0:T(8,128)}), (f32[4096,256]{0,1:T(8,128)}, f32[256,256]{1,0:T(8,128)})) %all-reduce.3.cloned.1.call-update) | async-done | bytes 4456464 | tf_op jit(solution)/shard_map/psum | solution.py:51
  146.5 1.6 select_reduce_fusion
  148.8 0.1 fusion.9
  148.9 13.2 %multiply_reduce_fusion.1 = (f32[]{:T(128)}, f32[4096,256]{0,1:T(8,128)S(1)}, f32[4096,256]{0,1:T(8,128)S(1)}) fusion(f32[4096,256]{0,1:T(8,128)} %copy.27, f32[4096]{0:T(1024)S(1)} %bitcast.30, f32[4096]{0:T(1024)S(1)} %bitcast.35, f32[4096,256]{0,1:T(8,128)} %get-tuple-element.12, f32[256,256]{1,0:T(8,128)} %get-tuple-element.13, f32[4096,256]{1,0:T(8,128)} %param.7), kind=kOutput, calls=%fused_computation.8 | convolution fusion | flops 3230662656 | bytes 21266436 | tf_op jit(solution)/shard_map/dot_general | solution.py:35
  162.1 7.4 %multiply_reduce_fusion = (f32[]{:T(128)}, f32[4096,256]{0,1:T(8,128)}, f32[4096,256]{0,1:T(8,128)S(1)}) fusion(f32[4096,256]{0,1:T(8,128)S(1)} %get-tuple-element.15, f32[4096]{0:T(1024)S(1)} %bitcast.32, f32[4096]{0:T(1024)S(1)} %bitcast.34, f32[4096,256]{0,1:T(8,128)S(1)} %copy-done.3, f32[256,256]{1,0:T(8,128)S(1)} %copy-done.4), kind=kOutput, calls=%fused_computation.7 | convolution fusion | flops 3230662656 | bytes 17072132 | tf_op jit(solution)/shard_map/dot_general | solution.py:35
  169.5 5.8 %fusion.8 = f32[]{:T(128)} fusion(f32[256,256]{1,0:T(8,128)S(1)} %copy-done.4, f32[4096,256]{0,1:T(8,128)S(1)} %get-tuple-element.15, f32[4096,256]{0,1:T(8,128)S(1)} %get-tuple-element.23, f32[4096]{0:T(1024)S(1)} %bitcast.33), kind=kOutput, calls=%fused_computation.18 | convolution fusion | flops 3227516928 | bytes 8667140 | tf_op jit(solution)/shard_map/dot_general | solution.py:40
  175.3 5.8 %fusion.7 = f32[]{:T(128)} fusion(f32[256,256]{1,0:T(8,128)S(1)} %copy-done.4, f32[4096,256]{0,1:T(8,128)S(1)} %copy-done.2, f32[4096,256]{0,1:T(8,128)S(1)} %get-tuple-element.22, f32[4096]{0:T(1024)S(1)} %bitcast.31), kind=kOutput, calls=%fused_computation.17 | convolution fusion | flops 3227516928 | bytes 8667140 | tf_op jit(solution)/shard_map/dot_general | solution.py:40
  181.1 2.7 maximum_bitcast_fusion
  183.8 0.6 broadcast_in_dim.11
  184.5 5.1 %all-to-all-start.1 = ((f32[8,2,2]{2,1,0:T(2,128)}), f32[8,2,2]{2,1,0:T(2,128)S(1)}, u32[]{:S(2)}, u32[]{:S(2)}) async-start(f32[8,2,2]{2,1,0:T(2,128)} %broadcast_in_dim.11), calls=%async_computation.1 | async-start | bytes 16384 | tf_op jit(solution)/shard_map/all_to_all | solution.py:9
  189.5 24.3 %fusion.16 = f32[4096,1536]{1,0:T(8,128)} fusion(f32[4096,256]{0,1:T(8,128)} %get-tuple-element.17, f32[256,1536]{1,0:T(8,128)S(1)} %copy-done), kind=kOutput, calls=%fused_computation.33 | convolution fusion | flops 19327352832 | bytes 30932992 | tf_op jit(solution)/shard_map/dot_general | solution.py:55
  213.8 27.5 %fusion = f32[256,1536]{1,0:T(8,128)} fusion(f32[4096,256]{0,1:T(8,128)} %get-tuple-element.17, f32[4096,1536]{1,0:T(8,128)} %fusion.16, f32[4096,1536]{1,0:T(8,128)} %param.5), kind=kOutput, calls=%fused_computation | convolution fusion | flops 19333644288 | bytes 56098816 | tf_op jit(solution)/shard_map/dot_general | solution.py:61
  241.4 4.8 %all-to-all-start = ((f32[8,32,1536]{2,1,0:T(8,128)}), f32[8,32,1536]{2,1,0:T(8,128)S(1)}, u32[]{:S(2)}, u32[]{:S(2)}) async-start(f32[8,32,1536]{2,1,0:T(8,128)} %bitcast.5), calls=%async_computation | async-start | bytes 3145728 | tf_op jit(solution)/shard_map/all_to_all | solution.py:24
  246.2 5.7 %copy.32 = f32[4096,256]{1,0:T(8,128)} copy(f32[4096,256]{0,1:T(8,128)} %get-tuple-element.17) | data formatting | bytes 8388608
  251.9 0.6 reduce_sum.70
  252.5 14.3 %all-to-all-done = f32[8,32,1536]{2,1,0:T(8,128)S(1)} async-done(((f32[8,32,1536]{2,1,0:T(8,128)}), f32[8,32,1536]{2,1,0:T(8,128)S(1)}, u32[]{:S(2)}, u32[]{:S(2)}) %all-to-all-start) | async-done | bytes 1572896 | tf_op jit(solution)/shard_map/all_to_all | solution.py:24
  266.7 0.8 reduce_sum.65
  (17 shorter events, 0.1 us)
Async XLA Ops:
  7.2 1.4 copy-start
  7.2 139.4 %all-reduce.3.cloned.1.call-start = ((), (), s32[]{:S(2)}) async-start(), calls=%async_computation.2 | async-start | bytes 8912896 | tf_op jit(solution)/shard_map/psum | solution.py:51
  37.2 0.8 copy-start.5
  37.9 5.6 %copy-start.6 = (s32[4096,2]{0,1:T(2,128)S(1)}, s32[4096,2]{0,1:T(2,128)}, u32[]{:S(2)}) copy-start(s32[4096,2]{0,1:T(2,128)} %param.8) | copy-start | bytes 98308
  148.9 13.2 %copy-start.3 = (f32[4096,256]{0,1:T(8,128)S(1)}, f32[4096,256]{0,1:T(8,128)}, u32[]{:S(2)}) copy-start(f32[4096,256]{0,1:T(8,128)} %get-tuple-element.12) | copy-start | bytes 12582916
  148.9 13.2 %copy-start.4 = (f32[256,256]{1,0:T(8,128)S(1)}, f32[256,256]{1,0:T(8,128)}, u32[]{:S(2)}) copy-start(f32[256,256]{1,0:T(8,128)} %get-tuple-element.13) | copy-start | bytes 786436
  169.5 5.8 %copy-start.2 = (f32[4096,256]{0,1:T(8,128)S(1)}, f32[4096,256]{0,1:T(8,128)}, u32[]{:S(2)}) copy-start(f32[4096,256]{0,1:T(8,128)} %copy.27) | copy-start | bytes 12582916
  184.5 56.9 %all-to-all-start.1 = ((f32[8,2,2]{2,1,0:T(2,128)}), f32[8,2,2]{2,1,0:T(2,128)S(1)}, u32[]{:S(2)}, u32[]{:S(2)}) async-start(f32[8,2,2]{2,1,0:T(2,128)} %broadcast_in_dim.11), calls=%async_computation.1 | async-start | bytes 16384 | tf_op jit(solution)/shard_map/all_to_all | solution.py:9
  241.4 25.4 %all-to-all-start = ((f32[8,32,1536]{2,1,0:T(8,128)}), f32[8,32,1536]{2,1,0:T(8,128)S(1)}, u32[]{:S(2)}, u32[]{:S(2)}) async-start(f32[8,32,1536]{2,1,0:T(8,128)} %bitcast.5), calls=%async_computation | async-start | bytes 3145728 | tf_op jit(solution)/shard_map/all_to_all | solution.py:24
  246.2 21.4 %copy-start.1 = (f32[256,1536]{1,0:T(8,128)S(1)}, f32[256,1536]{1,0:T(8,128)}, u32[]{:S(2)}) copy-start(f32[256,1536]{1,0:T(8,128)} %param.6) | copy-start | bytes 4718596
Sparse Core Ops, SparseCore 0:
  37.3 109.1 all-reduce.2
where the time goes:
time: 275 us; the launch traced here: 274 us
  waiting for transfers between devices  117 us (43%)
  matrix products  113 us (41%)
  between operations  14.8 us (5%)
  local copies, waits for them, and re-layouts  14.1 us (5%)
  starting transfers between devices  9.93 us (4%)
  other arithmetic  5.73 us (2%)
    psum x1, waiting for transfers between devices, per_device(): hh, ah = lax.psum((gram_part, ah_part), 'col')  103 us
    dot_general x1, matrix products, per_device(): lax.dot_general(columns, residue, (((0,), (0,)), ((), ())), precision=hig...  27.5 us
    dot_general x1, matrix products, per_device(): jnp.dot(a_matrix, h_factor.T, precision=highest, preferred_element_type=j...  26.4 us
    dot_general x1, matrix products, per_device(): jnp.dot(w_new, h_factor, precision=highest, preferred_element_type=jnp.fl...  24.3 us
    dot_general x2, matrix products, run_trials(): jnp.dot(current, hh, precision=highest, preferred_element_type=jnp.float32)  20.6 us
    all_to_all x1, waiting for transfers between devices, sum_at_owner(): parts = lax.all_to_all(cut_along(x, dim, peers), axis, 0, 0, tiled=True)  14.3 us
    unnamed x16, local copies, waits for them, and re-layouts  13.4 us
    dot_general x2, matrix products, run_trials(): jnp.dot(change, hh, precision=highest, preferred_element_type=jnp.float32)  11.7 us
  transfers between devices with their start and end apart: 3, of which 2 were waited for; matrix products, arithmetic and copies ran while one was open for 23% of the time, Pallas kernels for 0%

commit v1 on v0

v1 whole, which is shorter than its diff:
```python
import functools

import jax
import jax.numpy as jnp
from jax import lax
from jax.experimental import pallas as pl
from jax.experimental.pallas import tpu as pltpu
from jax.sharding import PartitionSpec as P

F32, BF16 = jnp.float32, jnp.bfloat16
MESH = pl.DeviceIdType.MESH
RANK, ROWS, COLS = 256, 4096, 1536
PIECE, GROUP, FLOW = 128, 512, 2048
TILES = 3
WIDTH = COLS // TILES
RELAY = (((2, 1), (3, 0)))


def halves(x):
    hi = x.astype(BF16)
    return hi, (x - hi.astype(F32)).astype(BF16)


def mm(a, b):
    return lax.dot_general(a, b, (((1,), (0,)), ((), ())), preferred_element_type=F32)


def exact(a, b):
    return jnp.dot(a, b, precision=lax.Precision.HIGHEST, preferred_element_type=F32)


def sem_keys():
    keys = []
    for f in range(2):
        for d in range(2):
            keys += [("ra", f, d, r) for r in RELAY[d]]
            keys += [("rb", f, d, r) for r in range(4)]
            keys += [("rc", f, d), ("rd", f, d, 0), ("rd", f, d, 1)]
            keys += [("g1", f, d), ("g1h", f, d)]
            keys += [("g2", f, d, r) for r in range(4)]
            keys += [("g2h", f, d, r) for r in range(4)]
    for name, count in (("s1", 4), ("s2", 4), ("s3", 4), ("s4", 8), ("a1", 8), ("a2", 4), ("a3", 4)):
        keys += [(name, d) for d in range(1, count)]
    for t in range(TILES):
        keys += [("core", t, k) for k in range(4)]
        for d in range(2):
            keys += [("ga", t, d), ("gb", t, d, 0), ("gb", t, d, 1)]
    return {key: at for at, key in enumerate(keys)}


KEYS = sem_keys()


def kernel(
    a_hbm, h_hbm, w_hbm, accept_hbm, shrink_hbm,
    w_out, g_out, stat_out,
    a_buf, a_hi, a_lo, h_f32, ht_hi, ht_lo, h_hi, h_lo,
    ah, ra, rb, rc, rd,
    gram, s1, s2, hh_buf,
    w_own, flags_raw, powers_raw, flags, factors, base,
    wg, acc, wtw, core_in, ga, gb, a1, a2, a3,
    send_sem, recv_sem, a_sem, in_sem, w_sem,
):
    rho, col = lax.axis_index("row"), lax.axis_index("col")
    y, z = lax.div(col, 4), lax.rem(col, 4)
    x, core = lax.div(rho, 2), lax.rem(rho, 2)
    along, across = (y, z), (z, y)

    def at_y(d):
        return (rho, lax.rem(y + d, 4) * 4 + z)

    def at_z(d):
        return (rho, y * 4 + lax.rem(z + d, 4))

    def at_row(d):
        return (lax.rem(rho + d, 8), col)

    def at_x(d):
        return (lax.rem(x + d, 4) * 2 + core, col)

    partner = (x * 2 + 1 - core, col)
    step_p, step_q = (at_y, at_z), (at_z, at_y)
    way = (1, 3)

    def row(f, dp, dq):
        return pl.multiple_of(
            f * FLOW + GROUP * lax.rem(along[f] + dp, 4) + PIECE * lax.rem(across[f] + dq, 4), PIECE
        )

    def piece(ref, f, dp, dq, start=0, size=PIECE):
        return ref.at[pl.ds(pl.multiple_of(row(f, dp, dq) + start, 64), size), :]

    sent = []

    def make(key, src, dst, to):
        return pltpu.make_async_remote_copy(
            src_ref=src, dst_ref=dst, send_sem=send_sem.at[KEYS[key]], recv_sem=recv_sem.at[KEYS[key]],
            device_id=to, device_id_type=MESH,
        )

    def send(key, src, dst, to):
        make(key, src(), dst(), to()).start()
        sent.append((key, src, dst, to))

    def arrived(key, dst, to):
        make(key, dst, dst, to).wait_recv()

    def chunk_row(j):
        f, t = lax.rem(j, 2), lax.div(j, 2)
        dp = 2 - t + 3 * lax.div(t, 2) - 2 * lax.div(t, 3)
        return pl.multiple_of(f * FLOW + GROUP * lax.rem(y + f * (z - y) + dp, 4), GROUP)

    def a_copy(j):
        slot = lax.rem(j, 2)
        return pltpu.make_async_copy(a_hbm.at[pl.ds(chunk_row(j), GROUP), :], a_buf.at[slot], a_sem.at[slot])

    h_copy = pltpu.make_async_copy(h_hbm, h_f32, in_sem.at[0])
    h_copy.start()
    a_copy(jnp.int32(0)).start()
    small = [
        pltpu.make_async_copy(accept_hbm, flags_raw, in_sem.at[1]),
        pltpu.make_async_copy(shrink_hbm, powers_raw, in_sem.at[2]),
        pltpu.make_async_copy(piece(w_hbm, 0, 0, 0), w_own.at[pl.ds(0, PIECE), :], in_sem.at[3]),
        pltpu.make_async_copy(piece(w_hbm, 1, 0, 0), w_own.at[pl.ds(PIECE, PIECE), :], in_sem.at[4]),
    ]
    for copy in small:
        copy.start()
    a_copy(jnp.int32(1)).start()

    barrier = pltpu.get_barrier_semaphore()
    peers = [at_row(d) for d in range(1, 8)] + [at_y(d) for d in range(1, 4)] + [at_z(d) for d in range(1, 4)]
    for peer in peers:
        pl.semaphore_signal(barrier, inc=1, device_id=peer, device_id_type=MESH)

    h_copy.wait()
    for n in range(COLS // 256):
        block = h_f32[:, n * 256 : (n + 1) * 256]
        hi, lo = halves(block)
        h_hi[:, n * 256 : (n + 1) * 256] = hi
        h_lo[:, n * 256 : (n + 1) * 256] = lo
        hi, lo = halves(block.T)
        ht_hi[n * 256 : (n + 1) * 256, :] = hi
        ht_lo[n * 256 : (n + 1) * 256, :] = lo
    part_hi, part_lo = halves(h_f32[pl.ds(pl.multiple_of(rho * 32, 32), 32), :])
    gram[...] = (
        mm(part_hi, ht_hi[...]) + mm(part_hi, ht_lo[...]) + mm(part_lo, ht_hi[...]) + mm(part_lo, ht_lo[...])
    )
    s1[y] = gram[pl.ds(pl.multiple_of(8 * y, 8), 8), :]
    pl.semaphore_wait(barrier, len(peers))

    def gram_rows(d):
        return gram.at[pl.ds(pl.multiple_of(8 * lax.rem(y + d, 4), 8), 8), :]

    for d in range(1, 4):
        send(("s1", d), lambda d=d: gram_rows(d), lambda: s1.at[y], lambda d=d: at_y(d))

    def gram_z():
        for d in range(1, 4):
            arrived(("s1", d), s1.at[lax.rem(y + 4 - d, 4)], at_y(d))
        s2[z] = s1[0] + s1[1] + s1[2] + s1[3]
        for d in range(1, 4):
            send(("s2", d), lambda: s2.at[z], lambda: s2.at[z], lambda d=d: at_z(d))

    def hh_rows(r, k):
        return hh_buf.at[r, pl.ds(pl.multiple_of(8 * k, 8), 8), :]

    def gram_y():
        for d in range(1, 4):
            arrived(("s2", d), s2.at[lax.rem(z + 4 - d, 4)], at_z(d))
        hh_buf[rho, pl.ds(pl.multiple_of(8 * y, 8), 8), :] = s2[0] + s2[1] + s2[2] + s2[3]
        for d in range(1, 4):
            send(("s3", d), lambda: hh_rows(rho, y), lambda: hh_rows(rho, y), lambda d=d: at_y(d))

    def gram_row():
        for d in range(1, 4):
            arrived(("s3", d), hh_rows(rho, lax.rem(y + 4 - d, 4)), at_y(d))
        for d in range(1, 8):
            send(("s4", d), lambda: hh_buf.at[rho], lambda: hh_buf.at[rho], lambda d=d: at_row(d))

    def opposite(f):
        for d in range(2):
            for i, r in enumerate(RELAY[d]):
                send(("ra", f, d, r), lambda r=r: piece(ah, f, 2, r), lambda d=d, i=i: ra.at[f, d, i],
                     lambda d=d: step_p[f](way[d]))

    def near(f, d, r):
        send(("rb", f, d, r), lambda: piece(ah, f, way[d], r), lambda: rb.at[f, d, r], lambda: step_p[f](way[d]))

    def alone(f, d):
        for r in RELAY[1 - d]:
            near(f, d, r)

    def relayed(f):
        for i in range(2):
            for d in range(2):
                r = RELAY[d][i]
                arrived(("ra", f, d, r), ra.at[f, d, i], step_p[f](way[d]))
                at = pl.ds(row(f, way[d], r), PIECE)
                ah[at, :] += ra[f, d, i]
                near(f, d, r)

    hooks = {
        0: [gram_z, lambda: opposite(0)],
        1: [lambda: opposite(1)],
        2: [gram_y, lambda: alone(0, 0)],
        3: [lambda: alone(1, 0)],
        4: [lambda: alone(0, 1)],
        5: [lambda: alone(1, 1), lambda: relayed(0)],
        6: [lambda: relayed(1), gram_row],
    }

    @pl.loop(0, 8)
    def _(j):
        slot = lax.rem(j, 2)
        at = pl.ds(chunk_row(j), GROUP)
        a_copy(j).wait()
        hi, lo = halves(a_buf[slot])
        a_hi[at, :] = hi
        a_lo[at, :] = lo

        @pl.when(j < 6)
        def _():
            a_copy(j + 2).start()

        ah[at, :] = mm(a_hi[at, :], ht_hi[...]) + mm(a_hi[at, :], ht_lo[...]) + mm(a_lo[at, :], ht_hi[...])
        for when, steps in hooks.items():

            @pl.when(j == when)
            def _(steps=steps):
                for step in steps:
                    step()

    for copy in small:
        copy.wait()
    acc[...] = jnp.zeros_like(acc)
    wtw[...] = jnp.zeros_like(wtw)

    def down(line):
        return jnp.broadcast_to(line, (PIECE, PIECE)).T

    for f in range(2):
        lanes = pl.ds(row(f, 0, 0), PIECE)
        for t in range(2):
            at = slice(f * PIECE, (f + 1) * PIECE)
            flags[t, at, :] = down(flags_raw[t : t + 1, lanes].astype(F32))
            power = powers_raw[t : t + 1, lanes]
            scale = jnp.where(power == 0, 1.0, jnp.where(power == 1, 0.5, jnp.where(power == 2, 0.25, 0.125)))
            factors[t, at, :] = down(scale.astype(F32))

    for d in range(1, 8):
        arrived(("s4", d), hh_buf.at[lax.rem(rho + 8 - d, 8)], at_row(d))
    hh = hh_buf[...].reshape(RANK, RANK)
    base[...] = exact(w_own[...], hh)

    def own_sum(f, r):
        for d in range(2):
            arrived(("rb", f, d, r), rb.at[f, d, r], step_p[f](way[d]))
        at = pl.ds(row(f, 0, r), PIECE)
        ah[at, :] += rb[f, 0, r] + rb[f, 1, r]

    def half(f, r, start):
        return lambda: piece(ah, f, 0, r, start, 64)

    for f in range(2):
        own_sum(f, 2)
        for d in range(2):
            send(("rc", f, d), half(f, 2, 64 * d), lambda f=f, d=d: rc.at[f, d], lambda f=f, d=d: step_q[f](way[d]))

    def last(f, d, part):
        start = 64 * d if part == 0 else 64 * (1 - d)
        send(("rd", f, d, part), half(f, way[d], start), lambda: rd.at[f, d, pl.ds(start, 64), :],
             lambda: step_q[f](way[d]))

    for d, r in ((1, 3), (0, 1)):
        for f in range(2):
            own_sum(f, r)
            last(f, d, 1)
    for f in range(2):
        own_sum(f, 0)
    for f in range(2):
        for d in range(2):
            arrived(("rc", f, d), rc.at[f, d], step_q[f](way[d]))
            at = pl.ds(pl.multiple_of(row(f, 0, way[d]) + 64 * d, 64), 64)
            ah[at, :] += rc[f, d]
            last(f, d, 0)
    for f in range(2):
        for d in range(2):
            for part in range(2):
                start = 64 * d if part == 0 else 64 * (1 - d)
                arrived(("rd", f, d, part), rd.at[f, d, pl.ds(start, 64), :], step_q[f](way[d]))
    own = [pl.ds(row(f, 0, 0), PIECE) for f in range(2)]
    total = jnp.concatenate([ah[own[f], :] + rd[f, 0] + rd[f, 1] for f in range(2)], axis=0)

    both = (RANK, RANK)
    eye = lax.broadcasted_iota(jnp.int32, both, 0) == lax.broadcasted_iota(jnp.int32, both, 1)
    step_size = float(RANK) / jnp.sum(jnp.where(eye, hh, 0.0), keepdims=True)

    def twice(v):
        return jnp.concatenate([v, v], axis=1)

    current = w_own[...]
    gradient = base[...] - total
    sums = []
    for t in range(2):
        change = jnp.maximum(current - twice(factors[t]) * step_size * gradient, 0.0) - current
        sums.append(jnp.sum(gradient * change, keepdims=True))
        current = current + twice(flags[t]) * change
        if t == 0:
            turned = exact(change, hh)
            sums.append(jnp.sum(change * turned, keepdims=True))
            gradient = gradient + twice(flags[t]) * turned
    for f in range(2):
        wg[own[f], :] = current[f * PIECE : (f + 1) * PIECE]

    for f in range(2):
        for d in range(2):
            send(("g1", f, d), lambda f=f: piece(wg, f, 0, 0), lambda f=f: piece(wg, f, 0, 0),
                 lambda f=f, d=d: step_q[f](way[d]))

    def spread(f, r):
        for d in range(2):
            send(("g2", f, d, r), lambda: piece(wg, f, 0, r), lambda: piece(wg, f, 0, r),
                 lambda d=d: step_p[f](way[d]))

    for f in range(2):
        spread(f, 0)
    sums.append(jnp.sum(change * exact(change, hh), keepdims=True))
    line = lax.broadcasted_iota(jnp.int32, (8, 128), 0)
    stats = jnp.zeros((8, 128), F32)
    for at, value in enumerate(sums):
        stats = jnp.where(line == at, value, stats)
    a1[rho] = stats
    for d in range(1, 8):
        send(("a1", d), lambda: a1.at[rho], lambda: a1.at[rho], lambda d=d: at_row(d))

    def stats_y():
        for d in range(1, 8):
            arrived(("a1", d), a1.at[lax.rem(rho + 8 - d, 8)], at_row(d))
        a2[y] = sum(a1[k] for k in range(1, 8)) + a1[0]
        for d in range(1, 4):
            send(("a2", d), lambda: a2.at[y], lambda: a2.at[y], lambda d=d: at_y(d))

    def stats_z():
        for d in range(1, 4):
            arrived(("a2", d), a2.at[lax.rem(y + 4 - d, 4)], at_y(d))
        a3[z] = a2[0] + a2[1] + a2[2] + a2[3]
        for d in range(1, 4):
            send(("a3", d), lambda: a3.at[z], lambda: a3.at[z], lambda d=d: at_z(d))

    def beside(f):
        for d in range(2):
            r = 4 - way[d]
            arrived(("g1", f, d), piece(wg, f, 0, r), step_q[f](way[d]))
            send(("g1h", f, d), lambda r=r, d=d: piece(wg, f, 0, r, 64 * d, 64),
                 lambda r=r, d=d: piece(wg, f, 0, r, 64 * d, 64), lambda d=d: step_q[f](way[d]))
        for r in (1, 3):
            spread(f, r)

    def across_ring(f):
        for d in range(2):
            arrived(("g1h", f, d), piece(wg, f, 0, 2, 64 * d, 64), step_q[f](way[d]))
        spread(f, 2)

    def onward(f, r):
        for d in range(2):
            dp = 4 - way[d]
            arrived(("g2", f, d, r), piece(wg, f, dp, r), step_p[f](way[d]))
            send(("g2h", f, d, r), lambda dp=dp, d=d: piece(wg, f, dp, r, 64 * d, 64),
                 lambda dp=dp, d=d: piece(wg, f, dp, r, 64 * d, 64), lambda d=d: step_p[f](way[d]))

    def far(f, r):
        for d in range(2):
            arrived(("g2h", f, d, r), piece(wg, f, 2, r, 64 * d, 64), step_p[f](way[d]))

    def w_copy(f, dp):
        at = pl.ds(pl.multiple_of(f * FLOW + GROUP * lax.rem(along[f] + dp, 4), GROUP), GROUP)
        return pltpu.make_async_copy(wg.at[at, :], w_out.at[at, :], w_sem.at[f * 4 + dp])

    def store(dp):
        for f in range(2):
            w_copy(f, dp).start()

    def pair(step, *given):
        return lambda: [step(f, *given) for f in range(2)]

    before = {
        1: [pair(beside)],
        2: [stats_y],
        3: [pair(across_ring), lambda: store(0)],
        4: [pair(onward, 0)],
        6: [pair(onward, 1)],
        8: [pair(onward, 3), stats_z],
        10: [pair(onward, 2), lambda: store(1), lambda: store(3)],
        12: [pair(far, 0)],
        13: [pair(far, 1)],
        14: [pair(far, 3)],
        15: [pair(far, 2), lambda: store(2)],
    }

    @pl.loop(0, 16)
    def _(u):
        for when, steps in before.items():

            @pl.when(u == when)
            def _(steps=steps):
                for step in steps:
                    step()

        e = lax.div(lax.div(u, 4) + 1, 2)
        e0, e1, e2 = 1 - lax.div(e + 1, 2), lax.rem(e, 2), lax.div(e, 2)
        dp = e1 * (1 + 2 * lax.rem(u, 2)) + e2 * 2
        k = e0 * u + e1 * lax.div(u - 4, 2) + e2 * (u - 12)
        r = k + lax.div(k, 2) - 2 * lax.div(k, 3)
        at = [pl.ds(row(f, dp, r), PIECE) for f in range(2)]

        w = jnp.concatenate([wg[at[0], :], wg[at[1], :]], axis=0)
        w_hi, w_lo = halves(w)
        t_hi, t_lo = halves(w.T)
        left = jnp.concatenate([t_hi, t_lo], axis=0)
        for t in range(TILES):
            cols = slice(t * WIDTH, (t + 1) * WIDTH)
            m_hi = jnp.concatenate([a_hi[at[0], cols], a_hi[at[1], cols]], axis=0)
            m_lo = jnp.concatenate([a_lo[at[0], cols], a_lo[at[1], cols]], axis=0)
            two = mm(left, m_hi)
            acc[t] += two[:RANK] + two[RANK:] + mm(t_hi, m_lo)
        two = mm(left, w_hi)
        wtw[...] += two[:RANK] + two[RANK:] + mm(t_hi, w_lo)

    def block(t, k, mine, start=0, size=32):
        at = 64 * lax.rem(x + k, 4) + 32 * (core if mine else 1 - core) + start
        return (t, pl.ds(pl.multiple_of(at, 16), size), slice(None))

    q_hi, q_lo = halves(wtw[...])

    def finish(t):
        cols = slice(t * WIDTH, (t + 1) * WIDTH)
        acc[t] = mm(q_hi, h_hi[:, cols]) + mm(q_hi, h_lo[:, cols]) + mm(q_lo, h_hi[:, cols]) - acc[t]
        for k in (2, 1, 3, 0):
            send(("core", t, k), lambda k=k: acc.at[block(t, k, False)], lambda k=k: core_in.at[t, k], lambda: partner)

    def joined(t, k):
        arrived(("core", t, k), core_in.at[t, k], partner)
        acc[block(t, k, True)] += core_in[t, k]

    def first(t):
        joined(t, 2)
        for d in range(2):
            send(("ga", t, d), lambda d=d: acc.at[block(t, 2, True, 16 * d, 16)], lambda d=d: ga.at[t, d],
                 lambda d=d: at_x(way[d]))
        for d in range(2):
            joined(t, way[d])
            onto(t, d, 1)
        joined(t, 0)

    def onto(t, d, part):
        start = 16 * d if part == 0 else 16 * (1 - d)
        send(("gb", t, d, part), lambda: acc.at[block(t, way[d], True, start, 16)],
             lambda: gb.at[t, d, pl.ds(start, 16), :], lambda: at_x(way[d]))

    def second(t):
        for d in range(2):
            arrived(("ga", t, d), ga.at[t, d], at_x(way[d]))
            acc[block(t, way[d], True, 16 * d, 16)] += ga[t, d]
            onto(t, d, 0)

    def third(t):
        for d in range(2):
            for part in range(2):
                start = 16 * d if part == 0 else 16 * (1 - d)
                arrived(("gb", t, d, part), gb.at[t, d, pl.ds(start, 16), :], at_x(way[d]))
        g_out[:, t * WIDTH : (t + 1) * WIDTH] = acc[block(t, 0, True)] + gb[t, 0] + gb[t, 1]

    for t in range(TILES):
        finish(t)
    for t in range(TILES):
        first(t)
    for t in range(TILES):
        second(t)
    for d in range(1, 4):
        arrived(("a3", d), a3.at[lax.rem(z + 4 - d, 4)], at_z(d))
    stat_out[...] = a3[0] + a3[1] + a3[2] + a3[3]
    for t in range(TILES):
        third(t)
    for f in range(2):
        for dp in range(4):
            w_copy(f, dp).wait()
    for key, src, dst, to in sent:
        make(key, src(), dst(), to()).wait_send()


def per_device(a_matrix, h_factor, w_factor, accept, shrink):
    vmem = pltpu.VMEM
    anywhere = pl.BlockSpec(memory_space=pl.ANY)
    inside = pl.BlockSpec(memory_space=vmem)
    w_new, grad_h, stats = pl.pallas_call(
        kernel,
        out_shape=(
            jax.ShapeDtypeStruct((ROWS, RANK), F32),
            jax.ShapeDtypeStruct((RANK // 8, COLS), F32),
            jax.ShapeDtypeStruct((8, 128), F32),
        ),
        in_specs=[anywhere] * 5,
        out_specs=(anywhere, inside, inside),
        scratch_shapes=[
            vmem((2, GROUP, COLS), F32),
            vmem((ROWS, COLS), BF16),
            vmem((ROWS, COLS), BF16),
            vmem((RANK, COLS), F32),
            vmem((COLS, RANK), BF16),
            vmem((COLS, RANK), BF16),
            vmem((RANK, COLS), BF16),
            vmem((RANK, COLS), BF16),
            vmem((ROWS, RANK), F32),
            vmem((2, 2, 2, PIECE, RANK), F32),
            vmem((2, 2, 4, PIECE, RANK), F32),
            vmem((2, 2, 64, RANK), F32),
            vmem((2, 2, PIECE, RANK), F32),
            vmem((32, RANK), F32),
            vmem((4, 8, RANK), F32),
            vmem((4, 8, RANK), F32),
            vmem((8, 32, RANK), F32),
            vmem((RANK, RANK), F32),
            vmem((2, ROWS), jnp.int32),
            vmem((2, ROWS), jnp.int32),
            vmem((2, RANK, PIECE), F32),
            vmem((2, RANK, PIECE), F32),
            vmem((RANK, RANK), F32),
            vmem((ROWS, RANK), F32),
            vmem((TILES, RANK, WIDTH), F32),
            vmem((RANK, RANK), F32),
            vmem((TILES, 4, 32, WIDTH), F32),
            vmem((TILES, 2, 16, WIDTH), F32),
            vmem((TILES, 2, 32, WIDTH), F32),
            vmem((8, 8, 128), F32),
            vmem((4, 8, 128), F32),
            vmem((4, 8, 128), F32),
            pltpu.SemaphoreType.DMA((len(KEYS),)),
            pltpu.SemaphoreType.DMA((len(KEYS),)),
            pltpu.SemaphoreType.DMA((2,)),
            pltpu.SemaphoreType.DMA((5,)),
            pltpu.SemaphoreType.DMA((8,)),
        ],
        compiler_params=pltpu.CompilerParams(
            collective_id=0, has_side_effects=True, vmem_limit_bytes=67043328
        ),
    )(a_matrix, h_factor, w_factor, accept.T, shrink.T)
    return w_new, grad_h, stats[:4, 0].reshape(2, 2)


def solution(mesh):
    in_specs = (P("row", "col"), P(None, "col"), P("row", None), P("row", None), P("row", None))
    out_specs = (P("row", None), P("row", "col"), P())
    return jax.shard_map(per_device, mesh=mesh, in_specs=in_specs, out_specs=out_specs, check_vma=False)
```

time: 275 us -> 90.2 us (0.33)
  waiting for transfers between devices: 117 us -> 0 us
  matrix products: 113 us -> 0 us
  Pallas kernels: 0 us -> 82.7 us
  between operations: 14.8 us -> 0.64 us
  starting transfers between devices: 9.93 us -> 0 us
  local copies, waits for them, and re-layouts: 14.1 us -> 6.63 us
  other arithmetic: 5.73 us -> 0 us
    dot_general x8 -> x0, matrix products: 113 us -> none  [the longest x1 27.5 us: per_device(): lax.dot_general(columns, residue, (((0,), (0,)), ((), ())), precision=hig...]
    psum x1 -> x0, waiting for transfers between devices: 103 us -> none  [per_device(): hh, ah = lax.psum((gram_part, ah_part), 'col')]
    pallas_call x0 -> x1, Pallas kernels: none -> 82.7 us  [per_device(): pl.pallas_call(kernel, out_shape=(jax.ShapeDtypeStruct((ROWS, RANK), F32)...]
    all_to_all x2 -> x0, waiting for transfers between devices: 14.3 us -> none  [the longest x1 14.3 us: sum_at_owner(): parts = lax.all_to_all(cut_along(x, dim, peers), axis, 0, 0, tiled=True)]
    all_to_all x2 -> x0, starting transfers between devices: 9.89 us -> none  [the longest x1 5.09 us: copy_for_each(): lax.all_to_all(jnp.broadcast_to(x[None], (peers, *x.shape)), axis, 0, 0,...]
    unnamed x16 -> x4, local copies, waits for them, and re-layouts: 13.4 us -> 5.19 us
    reduce_sum x3 -> x0, other arithmetic: 2.93 us -> none  [the longest x1 1.59 us: run_trials(): step_size = hh.shape[0] / jnp.trace(hh)]
  transfers between devices with their start and end apart: 3 -> 0, of which waited for: 2 -> 0; matrix products, arithmetic and copies ran while one was open for 23% -> 0% of each run, Pallas kernels for 0% -> 0%
where the time goes in v1:
time: 90.2 us; the launch traced here: 90 us
  Pallas kernels  82.7 us (92%)
  local copies, waits for them, and re-layouts  6.63 us (7%)
    pallas_call x1, Pallas kernels, per_device(): pl.pallas_call(kernel, out_shape=(jax.ShapeDtypeStruct((ROWS, RANK), F32)...  82.7 us
    unnamed x4, local copies, waits for them, and re-layouts  5.19 us

profile of v1, /device:TPU:1, one launch (start us, length us, event | category | flops | bytes accessed | tf_op | source)
XLA Modules:
  0.0 90.0 jit_solution(6048742284582240346)
XLA Ops:
  0.6 82.7 %shard_map.76 = (f32[4096,256]{1,0:T(8,128)}, f32[32,1536]{1,0:T(8,128)}, f32[8,128]{1,0:T(8,128)}) custom-call(f32[4096,1536]{1,0:T(8,128)} %a_hbm.1, f32[256,1536]{1,0:T(8,128)} %h_hbm.1, f32[4096,256]{1,0:T(8,128)} %w_hbm.1, s32[2,4096]{1,0:T(2,128)} %bitcast.2, s32[2,4096]{1,0:T(2,128)} %bitcast.3), custom_call_target="tpu_custom_call" | custom-call | tf_op jit(solution)/shard_map/pallas_call | solution.py:495
  83.4 0.8 slice_reduce_fusion
  84.2 0.6 reshape_squeeze.3
  84.8 0.0 copy-start
  84.8 4.5 %copy.10 = f32[4096,256]{1,0:T(8,128)} copy(f32[4096,256]{1,0:T(8,128)} %get-tuple-element.12) | data formatting | bytes 8388608
  89.3 0.0 copy-done
  89.3 0.7 copy.11
Async XLA Ops:
  84.8 4.5 %copy-start = (f32[32,1536]{1,0:T(8,128)S(1)}, f32[32,1536]{1,0:T(8,128)}, u32[]{:S(2)}) copy-start(f32[32,1536]{1,0:T(8,128)} %get-tuple-element.13) | copy-start | bytes 589828

commit v2 on v1

v2 whole, which is shorter than its diff:
```python
import functools

import jax
import jax.numpy as jnp
from jax import lax
from jax.experimental import pallas as pl
from jax.experimental.pallas import tpu as pltpu
from jax.sharding import PartitionSpec as P

F32, BF16 = jnp.float32, jnp.bfloat16
MESH = pl.DeviceIdType.MESH
RANK, ROWS, COLS = 256, 4096, 1536
PIECE, GROUP, FLOW = 128, 512, 2048
TILES = 3
WIDTH = COLS // TILES
RELAY = (((2, 1), (3, 0)))


def halves(x):
    hi = x.astype(BF16)
    return hi, (x - hi.astype(F32)).astype(BF16)


def mm(a, b):
    return lax.dot_general(a, b, (((1,), (0,)), ((), ())), preferred_element_type=F32)


def mmt(a, b):
    return lax.dot_general(a, b, (((1,), (1,)), ((), ())), preferred_element_type=F32)


def exact(a, b):
    return jnp.dot(a, b, precision=lax.Precision.HIGHEST, preferred_element_type=F32)


def sem_keys():
    keys = []
    for f in range(2):
        for d in range(2):
            keys += [("ra", f, d, r) for r in RELAY[d]]
            keys += [("rb", f, d, r) for r in range(4)]
            keys += [("rc", f, d), ("rd", f, d, 0), ("rd", f, d, 1)]
            keys += [("g1", f, d), ("g1h", f, d)]
            keys += [("g2", f, d, r) for r in range(4)]
            keys += [("g2h", f, d, r) for r in range(4)]
    for name, count in (("s1", 4), ("s2", 4), ("s4", 8), ("t1", 8), ("t2", 4), ("t3", 4), ("t4", 4), ("a1", 8), ("a2", 4), ("a3", 4)):
        keys += [(name, d) for d in range(1, count)]
    for t in range(TILES):
        keys += [("core", t, k) for k in range(4)]
        for d in range(2):
            keys += [("ga", t, d), ("gb", t, d, 0), ("gb", t, d, 1)]
    return {key: at for at, key in enumerate(keys)}


KEYS = sem_keys()


def kernel(
    a_hbm, h_hbm, w_hbm, accept_hbm, shrink_hbm,
    wg, g_out, stat_out,
    a_buf, a_hi, a_lo, h_f32, h_hi, h_lo,
    ah, ra, rb, rc, rd,
    s1, s2, t1, t_sum, t2, t3, t_all, hh_buf,
    w_own, flags_raw, powers_raw, flags, factors, base,
    acc, wtw, core_in, ga, gb, a1, a2, a3,
    send_sem, recv_sem, a_sem, in_sem,
):
    rho, col = lax.axis_index("row"), lax.axis_index("col")
    y, z = lax.div(col, 4), lax.rem(col, 4)
    x, core = lax.div(rho, 2), lax.rem(rho, 2)
    along, across = (y, z), (z, y)

    def at_y(d):
        return (rho, lax.rem(y + d, 4) * 4 + z)

    def at_z(d):
        return (rho, y * 4 + lax.rem(z + d, 4))

    def at_row(d):
        return (lax.rem(rho + d, 8), col)

    def at_x(d):
        return (lax.rem(x + d, 4) * 2 + core, col)

    partner = (x * 2 + 1 - core, col)
    step_p, step_q = (at_y, at_z), (at_z, at_y)
    way = (1, 3)

    def row(f, dp, dq):
        return pl.multiple_of(
            f * FLOW + GROUP * lax.rem(along[f] + dp, 4) + PIECE * lax.rem(across[f] + dq, 4), PIECE
        )

    def piece(ref, f, dp, dq, start=0, size=PIECE):
        return ref.at[pl.ds(pl.multiple_of(row(f, dp, dq) + start, 64), size), :]

    sent = []

    def make(key, src, dst, to):
        return pltpu.make_async_remote_copy(
            src_ref=src, dst_ref=dst, send_sem=send_sem.at[KEYS[key]], recv_sem=recv_sem.at[KEYS[key]],
            device_id=to, device_id_type=MESH,
        )

    def send(key, src, dst, to):
        make(key, src(), dst(), to()).start()
        sent.append((key, src, dst, to))

    def arrived(key, dst, to):
        make(key, dst, dst, to).wait_recv()

    def chunk_row(j):
        f, t = lax.rem(j, 2), lax.div(j, 2)
        dp = 2 - t + 3 * lax.div(t, 2) - 2 * lax.div(t, 3)
        return pl.multiple_of(f * FLOW + GROUP * lax.rem(y + f * (z - y) + dp, 4), GROUP)

    def a_copy(j):
        slot = lax.rem(j, 2)
        return pltpu.make_async_copy(a_hbm.at[pl.ds(chunk_row(j), GROUP), :], a_buf.at[slot], a_sem.at[slot])

    h_copy = pltpu.make_async_copy(h_hbm, h_f32, in_sem.at[0])
    h_copy.start()
    a_copy(jnp.int32(0)).start()
    small = [
        pltpu.make_async_copy(accept_hbm, flags_raw, in_sem.at[1]),
        pltpu.make_async_copy(shrink_hbm, powers_raw, in_sem.at[2]),
        pltpu.make_async_copy(piece(w_hbm, 0, 0, 0), w_own.at[pl.ds(0, PIECE), :], in_sem.at[3]),
        pltpu.make_async_copy(piece(w_hbm, 1, 0, 0), w_own.at[pl.ds(PIECE, PIECE), :], in_sem.at[4]),
    ]
    barrier = pltpu.get_barrier_semaphore()
    peers = [at_row(d) for d in range(1, 8)] + [at_y(d) for d in range(1, 4)] + [at_z(d) for d in range(1, 4)]
    for peer in peers:
        pl.semaphore_signal(barrier, inc=1, device_id=peer, device_id_type=MESH)

    h_copy.wait()
    hi, lo = halves(h_f32[...])
    h_hi[...] = hi
    h_lo[...] = lo
    a_copy(jnp.int32(1)).start()
    for copy in small:
        copy.start()
    part = jnp.concatenate(halves(h_f32[pl.ds(pl.multiple_of(rho * 32, 32), 32), :]), axis=0)
    two = mmt(part, h_hi[...]) + mmt(part, h_lo[...])
    s1[z] = two[:32] + two[32:]

    def greeted():
        pl.semaphore_wait(barrier, len(peers))
        for d in range(1, 4):
            send(("s1", d), lambda: s1.at[z], lambda: s1.at[z], lambda d=d: at_z(d))

    def gram_y():
        for d in range(1, 4):
            arrived(("s1", d), s1.at[lax.rem(z + 4 - d, 4)], at_z(d))
        s2[y] = s1[0] + s1[1] + s1[2] + s1[3]
        for d in range(1, 4):
            send(("s2", d), lambda: s2.at[y], lambda: s2.at[y], lambda d=d: at_y(d))

    def gram_row():
        for d in range(1, 4):
            arrived(("s2", d), s2.at[lax.rem(y + 4 - d, 4)], at_y(d))
        hh_buf[rho] = s2[0] + s2[1] + s2[2] + s2[3]
        for d in range(1, 8):
            send(("s4", d), lambda: hh_buf.at[rho], lambda: hh_buf.at[rho], lambda d=d: at_row(d))

    def opposite(f):
        for d in range(2):
            for i, r in enumerate(RELAY[d]):
                send(("ra", f, d, r), lambda r=r: piece(ah, f, 2, r), lambda d=d, i=i: ra.at[f, d, i],
                     lambda d=d: step_p[f](way[d]))

    def near(f, d, r):
        send(("rb", f, d, r), lambda: piece(ah, f, way[d], r), lambda: rb.at[f, d, r], lambda: step_p[f](way[d]))

    def relayed(f, d, r):
        i = RELAY[d].index(r)
        arrived(("ra", f, d, r), ra.at[f, d, i], step_p[f](way[d]))
        at = pl.ds(row(f, way[d], r), PIECE)
        ah[at, :] += ra[f, d, i]
        near(f, d, r)

    hooks = {
        0: [greeted, lambda: opposite(0)],
        1: [lambda: opposite(1)],
        2: [lambda: near(0, 0, 3)],
        3: [lambda: near(1, 0, 3), gram_y],
        4: [lambda: near(0, 1, 2), lambda: relayed(0, 0, 2)],
        5: [lambda: near(1, 1, 2), lambda: relayed(1, 0, 2), lambda: near(0, 1, 1), lambda: relayed(0, 0, 1)],
        6: [lambda: near(1, 1, 1), lambda: relayed(1, 0, 1), lambda: relayed(0, 1, 3)],
        7: [lambda: relayed(1, 1, 3), lambda: near(0, 0, 0), lambda: near(1, 0, 0)],
    }

    @pl.loop(0, 8)
    def _(j):
        slot = lax.rem(j, 2)
        at = pl.ds(chunk_row(j), GROUP)
        a_copy(j).wait()
        hi, lo = halves(a_buf[slot])
        a_hi[at, :] = hi
        a_lo[at, :] = lo

        @pl.when(j < 6)
        def _():
            a_copy(j + 2).start()

        ah[at, :] = mmt(a_hi[at, :], h_hi[...]) + mmt(a_hi[at, :], h_lo[...]) + mmt(a_lo[at, :], h_hi[...])
        for when, steps in hooks.items():

            @pl.when(j == when)
            def _(steps=steps):
                for step in steps:
                    step()

    def own_sum(f, r):
        for d in range(2):
            arrived(("rb", f, d, r), rb.at[f, d, r], step_p[f](way[d]))
        at = pl.ds(row(f, 0, r), PIECE)
        ah[at, :] += rb[f, 0, r] + rb[f, 1, r]

    def half(f, r, start):
        return lambda: piece(ah, f, 0, r, start, 64)

    def last(f, d, part):
        start = 64 * d if part == 0 else 64 * (1 - d)
        send(("rd", f, d, part), half(f, way[d], start), lambda: rd.at[f, d, pl.ds(start, 64), :],
             lambda: step_q[f](way[d]))

    for f in range(2):
        own_sum(f, 2)
        for d in range(2):
            send(("rc", f, d), half(f, 2, 64 * d), lambda f=f, d=d: rc.at[f, d], lambda f=f, d=d: step_q[f](way[d]))

    for f in range(2):
        relayed(f, 1, 0)
    gram_row()
    for copy in small:
        copy.wait()
    acc[...] = jnp.zeros_like(acc)
    def down(line):
        return jnp.broadcast_to(line, (PIECE, PIECE)).T

    for f in range(2):
        lanes = pl.ds(row(f, 0, 0), PIECE)
        for t in range(2):
            at = slice(f * PIECE, (f + 1) * PIECE)
            flags[t, at, :] = down(flags_raw[t : t + 1, lanes].astype(F32))
            power = powers_raw[t : t + 1, lanes]
            scale = jnp.where(power == 0, 1.0, jnp.where(power == 1, 0.5, jnp.where(power == 2, 0.25, 0.125)))
            factors[t, at, :] = down(scale.astype(F32))

    for d, r in ((0, 1), (1, 3)):
        for f in range(2):
            own_sum(f, r)
            last(f, d, 1)
    for f in range(2):
        for d in range(2):
            arrived(("rc", f, d), rc.at[f, d], step_q[f](way[d]))
            at = pl.ds(pl.multiple_of(row(f, 0, way[d]) + 64 * d, 64), 64)
            ah[at, :] += rc[f, d]
            last(f, d, 0)
    for d in range(1, 8):
        arrived(("s4", d), hh_buf.at[lax.rem(rho + 8 - d, 8)], at_row(d))
    hh = hh_buf[...].reshape(RANK, RANK)
    base[...] = exact(w_own[...], hh)

    for f in range(2):
        own_sum(f, 0)
    for f in range(2):
        for d in range(2):
            for part in range(2):
                start = 64 * d if part == 0 else 64 * (1 - d)
                arrived(("rd", f, d, part), rd.at[f, d, pl.ds(start, 64), :], step_q[f](way[d]))
    own = [pl.ds(row(f, 0, 0), PIECE) for f in range(2)]
    total = jnp.concatenate([ah[own[f], :] + rd[f, 0] + rd[f, 1] for f in range(2)], axis=0)

    both = (RANK, RANK)
    eye = lax.broadcasted_iota(jnp.int32, both, 0) == lax.broadcasted_iota(jnp.int32, both, 1)
    step_size = float(RANK) / jnp.sum(jnp.where(eye, hh, 0.0), keepdims=True)

    def twice(v):
        return jnp.concatenate([v, v], axis=1)

    current = w_own[...]
    gradient = base[...] - total
    sums = []
    for t in range(2):
        change = jnp.maximum(current - twice(factors[t]) * step_size * gradient, 0.0) - current
        sums.append(jnp.sum(gradient * change, keepdims=True))
        current = current + twice(flags[t]) * change
        if t == 0:
            turned = exact(change, hh)
            sums.append(jnp.sum(change * turned, keepdims=True))
            gradient = gradient + twice(flags[t]) * turned
    for f in range(2):
        wg[own[f], :] = current[f * PIECE : (f + 1) * PIECE]

    for f in range(2):
        for d in range(2):
            send(("g1", f, d), lambda f=f: piece(wg, f, 0, 0), lambda f=f: piece(wg, f, 0, 0),
                 lambda f=f, d=d: step_q[f](way[d]))

    def spread(f, r):
        for d in range(2):
            send(("g2", f, d, r), lambda: piece(wg, f, 0, r), lambda: piece(wg, f, 0, r),
                 lambda d=d: step_p[f](way[d]))

    sums.append(jnp.sum(change * exact(change, hh), keepdims=True))
    place = lax.broadcasted_iota(jnp.int32, (8, 128), 0) * 2 + lax.broadcasted_iota(jnp.int32, (8, 128), 1)
    stats = jnp.zeros((8, 128), F32)
    for at, value in enumerate(sums):
        stats = jnp.where(place == at, value, stats)
    a1[rho] = stats
    for d in range(1, 8):
        send(("a1", d), lambda: a1.at[rho], lambda: a1.at[rho], lambda d=d: at_row(d))

    c_hi, c_lo = halves(current)
    d_hi, d_lo = halves(current.T)
    wtw[...] = mm(d_hi, c_hi) + mm(d_lo, c_hi) + mm(d_hi, c_lo)

    def rows_of(ref, k, size):
        return ref.at[pl.ds(pl.multiple_of(size * k, size), size), :]

    for d in range(1, 8):
        send(("t1", d), lambda d=d: rows_of(wtw, lax.rem(rho + d, 8), 32), lambda: t1.at[rho], lambda d=d: at_row(d))

    def factor_z():
        t1[rho] = wtw[pl.ds(pl.multiple_of(32 * rho, 32), 32), :]
        for d in range(1, 8):
            arrived(("t1", d), t1.at[lax.rem(rho + 8 - d, 8)], at_row(d))
        rows = t1[0]
        for k in range(1, 8):
            rows = rows + t1[k]
        t_sum[...] = rows
        for d in range(1, 4):
            send(("t2", d), lambda d=d: rows_of(t_sum, lax.rem(z + d, 4), 8), lambda: t2.at[z], lambda d=d: at_z(d))

    def factor_y():
        t2[z] = t_sum[pl.ds(pl.multiple_of(8 * z, 8), 8), :]
        for d in range(1, 4):
            arrived(("t2", d), t2.at[lax.rem(z + 4 - d, 4)], at_z(d))
        t3[y] = t2[0] + t2[1] + t2[2] + t2[3]
        for d in range(1, 4):
            send(("t3", d), lambda: t3.at[y], lambda: t3.at[y], lambda d=d: at_y(d))

    def factor_all():
        for d in range(1, 4):
            arrived(("t3", d), t3.at[lax.rem(y + 4 - d, 4)], at_y(d))
        t_all[pl.ds(pl.multiple_of(8 * z, 8), 8), :] = t3[0] + t3[1] + t3[2] + t3[3]
        for d in range(1, 4):
            send(("t4", d), lambda: rows_of(t_all, z, 8), lambda: rows_of(t_all, z, 8), lambda d=d: at_z(d))

    def stats_y():
        for d in range(1, 8):
            arrived(("a1", d), a1.at[lax.rem(rho + 8 - d, 8)], at_row(d))
        a2[y] = sum(a1[k] for k in range(1, 8)) + a1[0]
        for d in range(1, 4):
            send(("a2", d), lambda: a2.at[y], lambda: a2.at[y], lambda d=d: at_y(d))

    def stats_z():
        for d in range(1, 4):
            arrived(("a2", d), a2.at[lax.rem(y + 4 - d, 4)], at_y(d))
        a3[z] = a2[0] + a2[1] + a2[2] + a2[3]
        for d in range(1, 4):
            send(("a3", d), lambda: a3.at[z], lambda: a3.at[z], lambda d=d: at_z(d))

    def beside(f):
        for d in range(2):
            r = 4 - way[d]
            arrived(("g1", f, d), piece(wg, f, 0, r), step_q[f](way[d]))
            send(("g1h", f, d), lambda r=r, d=d: piece(wg, f, 0, r, 64 * d, 64),
                 lambda r=r, d=d: piece(wg, f, 0, r, 64 * d, 64), lambda d=d: step_q[f](way[d]))

    def across_ring(f):
        for d in range(2):
            arrived(("g1h", f, d), piece(wg, f, 0, 2, 64 * d, 64), step_q[f](way[d]))
        spread(f, 2)

    def onward(f, r):
        for d in range(2):
            dp = 4 - way[d]
            arrived(("g2", f, d, r), piece(wg, f, dp, r), step_p[f](way[d]))
            send(("g2h", f, d, r), lambda dp=dp, d=d: piece(wg, f, dp, r, 64 * d, 64),
                 lambda dp=dp, d=d: piece(wg, f, dp, r, 64 * d, 64), lambda d=d: step_p[f](way[d]))

    def far(f, r):
        for d in range(2):
            arrived(("g2h", f, d, r), piece(wg, f, 2, r, 64 * d, 64), step_p[f](way[d]))

    def pair(step, *given):
        return lambda: [step(f, *given) for f in range(2)]

    before = {
        1: [pair(spread, 0), pair(beside)],
        2: [pair(spread, 1)],
        3: [pair(onward, 0)],
        4: [pair(spread, 3), stats_y, factor_z],
        5: [pair(across_ring)],
        6: [pair(onward, 1)],
        8: [pair(far, 0)],
        9: [pair(onward, 3), stats_z, factor_y],
        11: [pair(far, 1)],
        12: [pair(onward, 2)],
        14: [pair(far, 3), factor_all],
    }
    order = ((0, 0), (0, 1), (0, 3), (1, 0), (3, 0), (0, 2), (1, 1), (3, 1),
             (2, 0), (1, 3), (3, 3), (2, 1), (1, 2), (3, 2), (2, 3), (2, 2))
    codes = tuple(jnp.int32(sum((pair_[i] + 2) % 4 * 4**u for u, pair_ in enumerate(order))) for i in range(2))

    def factor_halves(at):
        return halves(jnp.concatenate([wg[at[0], :], wg[at[1], :]], axis=0).T)

    def gather(at, left, t):
        cols = slice(t * WIDTH, (t + 1) * WIDTH)
        m_hi = jnp.concatenate([a_hi[at[0], cols], a_hi[at[1], cols]], axis=0)
        m_lo = jnp.concatenate([a_lo[at[0], cols], a_lo[at[1], cols]], axis=0)
        acc[t] = acc[t] + mm(left[0], m_hi) + mm(left[1], m_hi) + mm(left[0], m_lo)

    def unit(u, codes):
        for when, steps in before.items():

            @pl.when(u == when)
            def _(steps=steps):
                for step in steps:
                    step()

        dp, r = lax.rem(codes[0], 4) + 2, lax.rem(codes[1], 4) + 2
        at = [pl.ds(row(f, dp, r), PIECE) for f in range(2)]

        left = factor_halves(at)
        for t in range(TILES):
            gather(at, left, t)
        return lax.div(codes[0], 4), lax.div(codes[1], 4)

    lax.fori_loop(0, 15, unit, codes)

    def block(t, k, mine, start=0, size=32):
        at = 64 * lax.rem(x + k, 4) + 32 * (core if mine else 1 - core) + start
        return (t, pl.ds(pl.multiple_of(at, 16), size), slice(None))

    def to_partner(t):
        for k in (2, 1, 3, 0):
            send(("core", t, k), lambda k=k: acc.at[block(t, k, False)], lambda k=k: core_in.at[t, k], lambda: partner)

    def joined(t, k):
        arrived(("core", t, k), core_in.at[t, k], partner)
        acc[block(t, k, True)] += core_in[t, k]

    def first(t):
        joined(t, 2)
        for d in range(2):
            send(("ga", t, d), lambda d=d: acc.at[block(t, 2, True, 16 * d, 16)], lambda d=d: ga.at[t, d],
                 lambda d=d: at_x(way[d]))

    def beyond(t):
        for d in range(2):
            joined(t, way[d])
            onto(t, d, 1)
        joined(t, 0)

    def onto(t, d, part):
        start = 16 * d if part == 0 else 16 * (1 - d)
        send(("gb", t, d, part), lambda: acc.at[block(t, way[d], True, start, 16)],
             lambda: gb.at[t, d, pl.ds(start, 16), :], lambda: at_x(way[d]))

    def second(t):
        for d in range(2):
            arrived(("ga", t, d), ga.at[t, d], at_x(way[d]))
            acc[block(t, way[d], True, 16 * d, 16)] += ga[t, d]
            onto(t, d, 0)

    def third(t):
        for d in range(2):
            for part in range(2):
                start = 16 * d if part == 0 else 16 * (1 - d)
                arrived(("gb", t, d, part), gb.at[t, d, pl.ds(start, 16), :], at_x(way[d]))
        g_out[:, t * WIDTH : (t + 1) * WIDTH] -= acc[block(t, 0, True)] + gb[t, 0] + gb[t, 1]

    def leave(items):
        for key, src, dst, to in items:
            make(key, src(), dst(), to()).wait_send()

    before_tail = list(sent)
    for f in range(2):
        far(f, 2)
    at = [pl.ds(row(f, 2, 2), PIECE) for f in range(2)]
    left = factor_halves(at)
    for t in range(TILES):
        gather(at, left, t)
        to_partner(t)
        if t > 0:
            first(t - 1)
    first(TILES - 1)
    for t in range(TILES):
        beyond(t)
    for d in range(1, 4):
        arrived(("t4", d), rows_of(t_all, lax.rem(z + 4 - d, 4), 8), at_z(d))
    t_hi, t_lo = halves(t_all[...])
    for t in range(TILES):
        cols = slice(t * WIDTH, (t + 1) * WIDTH)
        g_out[:, cols] = mm(t_hi, h_hi[:, cols]) + mm(t_hi, h_lo[:, cols]) + mm(t_lo, h_hi[:, cols])
    leave(before_tail)
    for t in range(TILES):
        second(t)
    for d in range(1, 4):
        arrived(("a3", d), a3.at[lax.rem(z + 4 - d, 4)], at_z(d))
    stat_out[...] = (a3[0] + a3[1] + a3[2] + a3[3])[:2, :2]
    for t in range(TILES):
        third(t)
    leave(sent[len(before_tail) :])


def per_device(a_matrix, h_factor, w_factor, accept, shrink):
    vmem = pltpu.VMEM
    anywhere = pl.BlockSpec(memory_space=pl.ANY)
    inside = pl.BlockSpec(memory_space=vmem)
    return pl.pallas_call(
        kernel,
        out_shape=(
            vmem((ROWS, RANK), F32),
            vmem((RANK // 8, COLS), F32),
            vmem((2, 2), F32),
        ),
        in_specs=[anywhere] * 5,
        out_specs=(inside, inside, inside),
        scratch_shapes=[
            vmem((2, GROUP, COLS), F32),
            vmem((ROWS, COLS), BF16),
            vmem((ROWS, COLS), BF16),
            vmem((RANK, COLS), F32),
            vmem((RANK, COLS), BF16),
            vmem((RANK, COLS), BF16),
            vmem((ROWS, RANK), F32),
            vmem((2, 2, 2, PIECE, RANK), F32),
            vmem((2, 2, 4, PIECE, RANK), F32),
            vmem((2, 2, 64, RANK), F32),
            vmem((2, 2, PIECE, RANK), F32),
            vmem((4, 32, RANK), F32),
            vmem((4, 32, RANK), F32),
            vmem((8, 32, RANK), F32),
            vmem((32, RANK), F32),
            vmem((4, 8, RANK), F32),
            vmem((4, 8, RANK), F32),
            vmem((32, RANK), F32),
            vmem((8, 32, RANK), F32),
            vmem((RANK, RANK), F32),
            vmem((2, ROWS), jnp.int32),
            vmem((2, ROWS), jnp.int32),
            vmem((2, RANK, PIECE), F32),
            vmem((2, RANK, PIECE), F32),
            vmem((RANK, RANK), F32),
            vmem((TILES, RANK, WIDTH), F32),
            vmem((RANK, RANK), F32),
            vmem((TILES, 4, 32, WIDTH), F32),
            vmem((TILES, 2, 16, WIDTH), F32),
            vmem((TILES, 2, 32, WIDTH), F32),
            vmem((8, 8, 128), F32),
            vmem((4, 8, 128), F32),
            vmem((4, 8, 128), F32),
            pltpu.SemaphoreType.DMA((len(KEYS),)),
            pltpu.SemaphoreType.DMA((len(KEYS),)),
            pltpu.SemaphoreType.DMA((2,)),
            pltpu.SemaphoreType.DMA((5,)),
        ],
        compiler_params=pltpu.CompilerParams(
            collective_id=0, has_side_effects=True, vmem_limit_bytes=58 * 1024 * 1024
        ),
    )(a_matrix, h_factor, w_factor, accept.T, shrink.T)

def solution(mesh):
    in_specs = (P("row", "col"), P(None, "col"), P("row", None), P("row", None), P("row", None))
    out_specs = (P("row", None), P("row", "col"), P())
    return jax.shard_map(per_device, mesh=mesh, in_specs=in_specs, out_specs=out_specs, check_vma=False)
```

time: 90.2 us -> 80 us (0.89)
  Pallas kernels: 82.7 us -> 75.9 us
  local copies, waits for them, and re-layouts: 6.63 us -> 3.25 us
    pallas_call x1, Pallas kernels: 82.7 us -> 75.9 us  [per_device(): pl.pallas_call(kernel, out_shape=(vmem((ROWS, RANK), F32), vmem((RANK //...]
    unnamed x4 -> x3, local copies, waits for them, and re-layouts: 5.19 us -> 3.25 us
where the time goes in v2:
time: 80 us; the launch traced here: 79.8 us
  Pallas kernels  75.9 us (95%)
  local copies, waits for them, and re-layouts  3.25 us (4%)
    pallas_call x1, Pallas kernels, per_device(): pl.pallas_call(kernel, out_shape=(vmem((ROWS, RANK), F32), vmem((RANK //...  75.9 us
    unnamed x3, local copies, waits for them, and re-layouts  3.25 us

profile of v2, /device:TPU:1, one launch (start us, length us, event | category | flops | bytes accessed | tf_op | source)
XLA Modules:
  0.0 79.8 jit_solution(15114221362796770428)
XLA Ops:
  0.6 75.9 %shard_map.76 = (f32[4096,256]{1,0:T(8,128)S(1)}, f32[32,1536]{1,0:T(8,128)S(1)}, f32[2,2]{1,0:T(2,128)S(1)}) custom-call(f32[4096,1536]{1,0:T(8,128)} %a_hbm.1, f32[256,1536]{1,0:T(8,128)} %h_hbm.1, f32[4096,256]{1,0:T(8,128)} %w_hbm.1, s32[2,4096]{1,0:T(2,128)} %bitcast.2, s32[2,4096]{1,0:T(2,128)} %bitcast.3), custom_call_target="tpu_custom_call" | custom-call | tf_op jit(solution)/shard_map/pallas_call | solution.py:515
  76.5 2.0 %copy.11 = f32[4096,256]{1,0:T(8,128)} copy(f32[4096,256]{1,0:T(8,128)S(1)} %get-tuple-element.3) | data formatting | bytes 8388608
  78.6 0.6 copy.13
  79.1 0.7 copy.12

commit v3 on v2

--- a/solution.py
+++ b/solution.py
@@ -61,7 +61,7 @@
     a_buf, a_hi, a_lo, h_f32, h_hi, h_lo,
     ah, ra, rb, rc, rd,
     s1, s2, t1, t_sum, t2, t3, t_all, hh_buf,
-    w_own, flags_raw, powers_raw, flags, factors, base,
+    w_own, flags_raw, powers_raw, flags, factors, base, updated,
     acc, wtw, core_in, ga, gb, a1, a2, a3,
     send_sem, recv_sem, a_sem, in_sem,
 ):
@@ -182,11 +182,11 @@
         0: [greeted, lambda: opposite(0)],
         1: [lambda: opposite(1)],
         2: [lambda: near(0, 0, 3)],
-        3: [lambda: near(1, 0, 3), gram_y],
-        4: [lambda: near(0, 1, 2), lambda: relayed(0, 0, 2)],
+        3: [lambda: near(1, 0, 3)],
+        4: [lambda: near(0, 1, 2), lambda: relayed(0, 0, 2), gram_y],
         5: [lambda: near(1, 1, 2), lambda: relayed(1, 0, 2), lambda: near(0, 1, 1), lambda: relayed(0, 0, 1)],
         6: [lambda: near(1, 1, 1), lambda: relayed(1, 0, 1), lambda: relayed(0, 1, 3)],
-        7: [lambda: relayed(1, 1, 3), lambda: near(0, 0, 0), lambda: near(1, 0, 0)],
+        7: [lambda: relayed(1, 1, 3)],
     }
 
     @pl.loop(0, 8)
@@ -230,6 +230,7 @@
             send(("rc", f, d), half(f, 2, 64 * d), lambda f=f, d=d: rc.at[f, d], lambda f=f, d=d: step_q[f](way[d]))
 
     for f in range(2):
+        near(f, 0, 0)
         relayed(f, 1, 0)
     gram_row()
     for copy in small:
@@ -264,46 +265,49 @@
 
     for f in range(2):
         own_sum(f, 0)
-    for f in range(2):
+    own = [pl.ds(row(f, 0, 0), PIECE) for f in range(2)]
+
+    both = (RANK, RANK)
+    eye = lax.broadcasted_iota(jnp.int32, both, 0) == lax.broadcasted_iota(jnp.int32, both, 1)
+    step_size = float(RANK) / jnp.sum(jnp.where(eye, hh, 0.0), keepdims=True)
+
+    def twice(v):
+        return jnp.concatenate([v, v], axis=1)
+
+    def trials(f):
         for d in range(2):
             for part in range(2):
                 start = 64 * d if part == 0 else 64 * (1 - d)
                 arrived(("rd", f, d, part), rd.at[f, d, pl.ds(start, 64), :], step_q[f](way[d]))
-    own = [pl.ds(row(f, 0, 0), PIECE) for f in range(2)]
-    total = jnp.concatenate([ah[own[f], :] + rd[f, 0] + rd[f, 1] for f in range(2)], axis=0)
-
-    both = (RANK, RANK)
-    eye = lax.broadcasted_iota(jnp.int32, both, 0) == lax.broadcasted_iota(jnp.int32, both, 1)
-    step_size = float(RANK) / jnp.sum(jnp.where(eye, hh, 0.0), keepdims=True)
-
-    def twice(v):
-        return jnp.concatenate([v, v], axis=1)
-
-    current = w_own[...]
-    gradient = base[...] - total
-    sums = []
-    for t in range(2):
-        change = jnp.maximum(current - twice(factors[t]) * step_size * gradient, 0.0) - current
-        sums.append(jnp.sum(gradient * change, keepdims=True))
-        current = current + twice(flags[t]) * change
-        if t == 0:
-            turned = exact(change, hh)
-            sums.append(jnp.sum(change * turned, keepdims=True))
-            gradient = gradient + twice(flags[t]) * turned
-    for f in range(2):
-        wg[own[f], :] = current[f * PIECE : (f + 1) * PIECE]
-
-    for f in range(2):
-        for d in range(2):
-            send(("g1", f, d), lambda f=f: piece(wg, f, 0, 0), lambda f=f: piece(wg, f, 0, 0),
-                 lambda f=f, d=d: step_q[f](way[d]))
+        at = slice(f * PIECE, (f + 1) * PIECE)
+        current = w_own[at, :]
+        gradient = base[at, :] - (ah[own[f], :] + rd[f, 0] + rd[f, 1])
+        sums = []
+        for t in range(2):
+            change = jnp.maximum(current - twice(factors[t, at, :]) * step_size * gradient, 0.0) - current
+            sums.append(jnp.sum(gradient * change, keepdims=True))
+            current = current + twice(flags[t, at, :]) * change
+            if t == 0:
+                turned = exact(change, hh)
+                sums.append(jnp.sum(change * turned, keepdims=True))
+                gradient = gradient + twice(flags[t, at, :]) * turned
+        wg[own[f], :] = current
+        for d in range(2):
+            send(("g1", f, d), lambda: piece(wg, f, 0, 0), lambda: piece(wg, f, 0, 0),
+                 lambda d=d: step_q[f](way[d]))
+        updated[at, :] = current
+        return sums, change
 
     def spread(f, r):
         for d in range(2):
             send(("g2", f, d, r), lambda: piece(wg, f, 0, r), lambda: piece(wg, f, 0, r),
                  lambda d=d: step_p[f](way[d]))
 
-    sums.append(jnp.sum(change * exact(change, hh), keepdims=True))
+    made = [trials(0), trials(1)]
+    spread(0, 0)
+    ends = jnp.concatenate([change for _, change in made], axis=0)
+    sums = [first_ + second_ for first_, second_ in zip(made[0][0], made[1][0])]
+    sums.append(jnp.sum(ends * exact(ends, hh), keepdims=True))
     place = lax.broadcasted_iota(jnp.int32, (8, 128), 0) * 2 + lax.broadcasted_iota(jnp.int32, (8, 128), 1)
     stats = jnp.zeros((8, 128), F32)
     for at, value in enumerate(sums):
@@ -312,6 +316,7 @@
     for d in range(1, 8):
         send(("a1", d), lambda: a1.at[rho], lambda: a1.at[rho], lambda d=d: at_row(d))
 
+    current = updated[...]
     c_hi, c_lo = halves(current)
     d_hi, d_lo = halves(current.T)
     wtw[...] = mm(d_hi, c_hi) + mm(d_lo, c_hi) + mm(d_hi, c_lo)
@@ -374,10 +379,13 @@
             arrived(("g1h", f, d), piece(wg, f, 0, 2, 64 * d, 64), step_q[f](way[d]))
         spread(f, 2)
 
+    def come(f, r):
+        for d in range(2):
+            arrived(("g2", f, d, r), piece(wg, f, 4 - way[d], r), step_p[f](way[d]))
+
     def onward(f, r):
         for d in range(2):
             dp = 4 - way[d]
-            arrived(("g2", f, d, r), piece(wg, f, dp, r), step_p[f](way[d]))
             send(("g2h", f, d, r), lambda dp=dp, d=d: piece(wg, f, dp, r, 64 * d, 64),
                  lambda dp=dp, d=d: piece(wg, f, dp, r, 64 * d, 64), lambda d=d: step_p[f](way[d]))
 
@@ -389,30 +397,31 @@
         return lambda: [step(f, *given) for f in range(2)]
 
     before = {
-        1: [pair(spread, 0), pair(beside)],
-        2: [pair(spread, 1)],
-        3: [pair(onward, 0)],
-        4: [pair(spread, 3), stats_y, factor_z],
-        5: [pair(across_ring)],
-        6: [pair(onward, 1)],
-        8: [pair(far, 0)],
-        9: [pair(onward, 3), stats_z, factor_y],
-        11: [pair(far, 1)],
-        12: [pair(onward, 2)],
-        14: [pair(far, 3), factor_all],
+        0: [lambda: spread(1, 0), pair(beside), pair(spread, 1), pair(spread, 3)],
+        1: [pair(come, 0)],
+        2: [pair(across_ring), stats_y, factor_z, pair(onward, 0)],
+        3: [pair(come, 1), pair(onward, 1)],
+        4: [pair(come, 3), pair(onward, 3)],
+        5: [pair(come, 2), pair(onward, 2), stats_z, factor_y],
+        6: [pair(far, 0), pair(far, 1)],
+        7: [pair(far, 3), pair(far, 2)],
     }
-    order = ((0, 0), (0, 1), (0, 3), (1, 0), (3, 0), (0, 2), (1, 1), (3, 1),
-             (2, 0), (1, 3), (3, 3), (2, 1), (1, 2), (3, 2), (2, 3), (2, 2))
-    codes = tuple(jnp.int32(sum((pair_[i] + 2) % 4 * 4**u for u, pair_ in enumerate(order))) for i in range(2))
+    order = (((0, 0), (0, 1)), ((1, 0), (3, 0)), ((0, 3), (0, 2)), ((1, 1), (3, 1)),
+             ((1, 3), (3, 3)), ((1, 2), (3, 2)), ((2, 0), (2, 1)), ((2, 3), (2, 2)))
+    codes = tuple(
+        jnp.int32(sum(cell[n][i] * 4**u for u, cell in enumerate(order))) for n in range(2) for i in range(2)
+    )
 
     def factor_halves(at):
-        return halves(jnp.concatenate([wg[at[0], :], wg[at[1], :]], axis=0).T)
-
-    def gather(at, left, t):
-        cols = slice(t * WIDTH, (t + 1) * WIDTH)
-        m_hi = jnp.concatenate([a_hi[at[0], cols], a_hi[at[1], cols]], axis=0)
-        m_lo = jnp.concatenate([a_lo[at[0], cols], a_lo[at[1], cols]], axis=0)
-        acc[t] = acc[t] + mm(left[0], m_hi) + mm(left[1], m_hi) + mm(left[0], m_lo)
+        return halves(jnp.concatenate([wg[rows, :] for rows in at], axis=0).T)
+
+    def block(t, k, mine, start=0, size=32):
+        at = 64 * lax.rem(x + k, 4) + 32 * (core if mine else 1 - core) + start
+        return (t, pl.ds(pl.multiple_of(at, 16), size), slice(None))
+
+    def to_partner(t):
+        for k in (2, 1, 3, 0):
+            send(("core", t, k), lambda k=k: acc.at[block(t, k, False)], lambda k=k: core_in.at[t, k], lambda: partner)
 
     def unit(u, codes):
         for when, steps in before.items():
@@ -422,23 +431,19 @@
                 for step in steps:
                     step()
 
-        dp, r = lax.rem(codes[0], 4) + 2, lax.rem(codes[1], 4) + 2
-        at = [pl.ds(row(f, dp, r), PIECE) for f in range(2)]
-
-        left = factor_halves(at)
+        at = []
+        for n in range(2):
+            dp, r = lax.rem(codes[2 * n], 4), lax.rem(codes[2 * n + 1], 4)
+            at += [pl.ds(row(f, dp, r), PIECE) for f in range(2)]
+        left_hi, left_lo = factor_halves(at)
         for t in range(TILES):
-            gather(at, left, t)
-        return lax.div(codes[0], 4), lax.div(codes[1], 4)
-
-    lax.fori_loop(0, 15, unit, codes)
-
-    def block(t, k, mine, start=0, size=32):
-        at = 64 * lax.rem(x + k, 4) + 32 * (core if mine else 1 - core) + start
-        return (t, pl.ds(pl.multiple_of(at, 16), size), slice(None))
-
-    def to_partner(t):
-        for k in (2, 1, 3, 0):
-            send(("core", t, k), lambda k=k: acc.at[block(t, k, False)], lambda k=k: core_in.at[t, k], lambda: partner)
+            cols = slice(t * WIDTH, (t + 1) * WIDTH)
+            m_hi = jnp.concatenate([a_hi[rows, cols] for rows in at], axis=0)
+            m_lo = jnp.concatenate([a_lo[rows, cols] for rows in at], axis=0)
+            acc[t] = acc[t] + mm(left_hi, m_hi) + mm(left_lo, m_hi) + mm(left_hi, m_lo)
+        return tuple(lax.div(code, 4) for code in codes)
+
+    lax.fori_loop(0, 8, unit, codes)
 
     def joined(t, k):
         arrived(("core", t, k), core_in.at[t, k], partner)
@@ -479,27 +484,22 @@
             make(key, src(), dst(), to()).wait_send()
 
     before_tail = list(sent)
-    for f in range(2):
-        far(f, 2)
-    at = [pl.ds(row(f, 2, 2), PIECE) for f in range(2)]
-    left = factor_halves(at)
-    for t in range(TILES):
-        gather(at, left, t)
+    for t in range(TILES):
         to_partner(t)
-        if t > 0:
-            first(t - 1)
-    first(TILES - 1)
+    for t in range(TILES):
+        first(t)
     for t in range(TILES):
         beyond(t)
+    factor_all()
+    for t in range(TILES):
+        second(t)
+    leave(before_tail)
     for d in range(1, 4):
         arrived(("t4", d), rows_of(t_all, lax.rem(z + 4 - d, 4), 8), at_z(d))
     t_hi, t_lo = halves(t_all[...])
     for t in range(TILES):
         cols = slice(t * WIDTH, (t + 1) * WIDTH)
         g_out[:, cols] = mm(t_hi, h_hi[:, cols]) + mm(t_hi, h_lo[:, cols]) + mm(t_lo, h_hi[:, cols])
-    leave(before_tail)
-    for t in range(TILES):
-        second(t)
     for d in range(1, 4):
         arrived(("a3", d), a3.at[lax.rem(z + 4 - d, 4)], at_z(d))
     stat_out[...] = (a3[0] + a3[1] + a3[2] + a3[3])[:2, :2]
@@ -547,6 +547,7 @@
             vmem((2, RANK, PIECE), F32),
             vmem((2, RANK, PIECE), F32),
             vmem((RANK, RANK), F32),
+            vmem((RANK, RANK), F32),
             vmem((TILES, RANK, WIDTH), F32),
             vmem((RANK, RANK), F32),
             vmem((TILES, 4, 32, WIDTH), F32),

time: 80 us -> 76.9 us (0.961)
  Pallas kernels: 75.9 us -> 72.8 us
    pallas_call x1, Pallas kernels: 75.9 us -> 72.8 us  [per_device(): pl.pallas_call(kernel, out_shape=(vmem((ROWS, RANK), F32), vmem((RANK //...]
where the time goes in v3:
time: 76.9 us; the launch traced here: 76.7 us
  Pallas kernels  72.8 us (95%)
  local copies, waits for them, and re-layouts  3.25 us (4%)
    pallas_call x1, Pallas kernels, per_device(): pl.pallas_call(kernel, out_shape=(vmem((ROWS, RANK), F32), vmem((RANK //...  72.8 us
    unnamed x3, local copies, waits for them, and re-layouts  3.25 us

profile of v3, /device:TPU:1, one launch (start us, length us, event | category | flops | bytes accessed | tf_op | source)
XLA Modules:
  0.0 76.7 jit_solution(3566529165252651848)
XLA Ops:
  0.6 72.8 %shard_map.76 = (f32[4096,256]{1,0:T(8,128)S(1)}, f32[32,1536]{1,0:T(8,128)S(1)}, f32[2,2]{1,0:T(2,128)S(1)}) custom-call(f32[4096,1536]{1,0:T(8,128)} %a_hbm.1, f32[256,1536]{1,0:T(8,128)} %h_hbm.1, f32[4096,256]{1,0:T(8,128)} %w_hbm.1, s32[2,4096]{1,0:T(2,128)} %bitcast.2, s32[2,4096]{1,0:T(2,128)} %bitcast.3), custom_call_target="tpu_custom_call" | custom-call | tf_op jit(solution)/shard_map/pallas_call | solution.py:515
  73.4 2.0 %copy.11 = f32[4096,256]{1,0:T(8,128)} copy(f32[4096,256]{1,0:T(8,128)S(1)} %get-tuple-element.3) | data formatting | bytes 8388608
  75.4 0.6 copy.13
  76.0 0.7 copy.12

commit v4 on v3

--- a/solution.py
+++ b/solution.py
@@ -304,7 +304,6 @@
                  lambda d=d: step_p[f](way[d]))
 
     made = [trials(0), trials(1)]
-    spread(0, 0)
     ends = jnp.concatenate([change for _, change in made], axis=0)
     sums = [first_ + second_ for first_, second_ in zip(made[0][0], made[1][0])]
     sums.append(jnp.sum(ends * exact(ends, hh), keepdims=True))
@@ -397,7 +396,7 @@
         return lambda: [step(f, *given) for f in range(2)]
 
     before = {
-        0: [lambda: spread(1, 0), pair(beside), pair(spread, 1), pair(spread, 3)],
+        0: [pair(spread, 0), pair(beside), pair(spread, 1), pair(spread, 3)],
         1: [pair(come, 0)],
         2: [pair(across_ring), stats_y, factor_z, pair(onward, 0)],
         3: [pair(come, 1), pair(onward, 1)],
@@ -508,11 +507,22 @@
     leave(sent[len(before_tail) :])
 
 
+def hand_over(w_in, g_in, stat_in, w_out, g_out, stat_out, out_sem):
+    copies = [
+        pltpu.make_async_copy(source, target, out_sem.at[n])
+        for n, (source, target) in enumerate(((w_in, w_out), (g_in, g_out), (stat_in, stat_out)))
+    ]
+    for copy in copies:
+        copy.start()
+    for copy in copies:
+        copy.wait()
+
+
 def per_device(a_matrix, h_factor, w_factor, accept, shrink):
     vmem = pltpu.VMEM
     anywhere = pl.BlockSpec(memory_space=pl.ANY)
     inside = pl.BlockSpec(memory_space=vmem)
-    return pl.pallas_call(
+    results = pl.pallas_call(
         kernel,
         out_shape=(
             vmem((ROWS, RANK), F32),
@@ -565,6 +575,19 @@
             collective_id=0, has_side_effects=True, vmem_limit_bytes=58 * 1024 * 1024
         ),
     )(a_matrix, h_factor, w_factor, accept.T, shrink.T)
+    held = [pltpu.with_memory_space_constraint(result, vmem) for result in results]
+    return pl.pallas_call(
+        hand_over,
+        out_shape=(
+            jax.ShapeDtypeStruct((ROWS, RANK), F32),
+            jax.ShapeDtypeStruct((RANK // 8, COLS), F32),
+            jax.ShapeDtypeStruct((2, 2), F32),
+        ),
+        in_specs=[inside, inside, inside],
+        out_specs=(anywhere, anywhere, anywhere),
+        scratch_shapes=[pltpu.SemaphoreType.DMA((3,))],
+        compiler_params=pltpu.CompilerParams(vmem_limit_bytes=8 * 1024 * 1024),
+    )(*held)
 
 def solution(mesh):
     in_specs = (P("row", "col"), P(None, "col"), P("row", None), P("row", None), P("row", None))

time: 76.9 us -> 75.8 us (0.986)
  local copies, waits for them, and re-layouts: 3.25 us -> 0 us
  Pallas kernels: 72.8 us -> 74.9 us
    unnamed x3 -> x0, local copies, waits for them, and re-layouts: 3.25 us -> none
    pallas_call x0 -> x1, Pallas kernels: none -> 2.09 us  [per_device(): pl.pallas_call(hand_over, out_shape=(jax.ShapeDtypeStruct((ROWS, RANK), F...]
where the time goes in v4:
time: 75.8 us; the launch traced here: 75.5 us
  Pallas kernels  74.9 us (99%)
    pallas_call x1, Pallas kernels, per_device(): pl.pallas_call(kernel, out_shape=(vmem((ROWS, RANK), F32), vmem((RANK //...  72.8 us
    pallas_call x1, Pallas kernels, per_device(): pl.pallas_call(hand_over, out_shape=(jax.ShapeDtypeStruct((ROWS, RANK), F...  2.09 us

profile of v4, /device:TPU:1, one launch (start us, length us, event | category | flops | bytes accessed | tf_op | source)
XLA Modules:
  0.0 75.5 jit_solution(16865595951760813794)
XLA Ops:
  0.6 72.8 %shard_map.76 = (f32[4096,256]{1,0:T(8,128)S(1)}, f32[32,1536]{1,0:T(8,128)S(1)}, f32[2,2]{1,0:T(2,128)S(1)}) custom-call(f32[4096,1536]{1,0:T(8,128)} %a_hbm.1, f32[256,1536]{1,0:T(8,128)} %h_hbm.1, f32[4096,256]{1,0:T(8,128)} %w_hbm.1, s32[2,4096]{1,0:T(2,128)} %bitcast.2, s32[2,4096]{1,0:T(2,128)} %bitcast.3), custom_call_target="tpu_custom_call" | custom-call | tf_op jit(solution)/shard_map/pallas_call | solution.py:525
  73.4 2.1 %shard_map.77 = (f32[4096,256]{1,0:T(8,128)}, f32[32,1536]{1,0:T(8,128)}, f32[2,2]{1,0:T(2,128)}) custom-call(f32[4096,256]{1,0:T(8,128)S(1)} %get-tuple-element.6.w_in, f32[32,1536]{1,0:T(8,128)S(1)} %get-tuple-element.7.g_in, f32[2,2]{1,0:T(2,128)S(1)} %get-tuple-element.8.stat_in), custom_call_target="tpu_custom_call" | custom-call | tf_op jit(solution)/shard_map/pallas_call | solution.py:579

commit v5 on v4

--- a/solution.py
+++ b/solution.py
@@ -11,7 +11,7 @@
 MESH = pl.DeviceIdType.MESH
 RANK, ROWS, COLS = 256, 4096, 1536
 PIECE, GROUP, FLOW = 128, 512, 2048
-TILES = 3
+TILES = 1
 WIDTH = COLS // TILES
 RELAY = (((2, 1), (3, 0)))
 

time: 75.8 us -> 75.3 us (level)
  no operation moved by 1% of the time
where the time goes in v5:
time: 75.3 us; the launch traced here: 75.1 us
  Pallas kernels  74.5 us (99%)
    pallas_call x1, Pallas kernels, per_device(): pl.pallas_call(kernel, out_shape=(vmem((ROWS, RANK), F32), vmem((RANK //...  72.4 us
    pallas_call x1, Pallas kernels, per_device(): pl.pallas_call(hand_over, out_shape=(jax.ShapeDtypeStruct((ROWS, RANK), F...  2.09 us

profile of v5, /device:TPU:1, one launch (start us, length us, event | category | flops | bytes accessed | tf_op | source)
XLA Modules:
  0.0 75.1 jit_solution(2432810189560707818)
XLA Ops:
  0.6 72.4 %shard_map.76 = (f32[4096,256]{1,0:T(8,128)S(1)}, f32[32,1536]{1,0:T(8,128)S(1)}, f32[2,2]{1,0:T(2,128)S(1)}) custom-call(f32[4096,1536]{1,0:T(8,128)} %a_hbm.1, f32[256,1536]{1,0:T(8,128)} %h_hbm.1, f32[4096,256]{1,0:T(8,128)} %w_hbm.1, s32[2,4096]{1,0:T(2,128)} %bitcast.2, s32[2,4096]{1,0:T(2,128)} %bitcast.3), custom_call_target="tpu_custom_call" | custom-call | tf_op jit(solution)/shard_map/pallas_call | solution.py:525
  73.0 2.1 %shard_map.77 = (f32[4096,256]{1,0:T(8,128)}, f32[32,1536]{1,0:T(8,128)}, f32[2,2]{1,0:T(2,128)}) custom-call(f32[4096,256]{1,0:T(8,128)S(1)} %get-tuple-element.6.w_in, f32[32,1536]{1,0:T(8,128)S(1)} %get-tuple-element.7.g_in, f32[2,2]{1,0:T(2,128)S(1)} %get-tuple-element.8.stat_in), custom_call_target="tpu_custom_call" | custom-call | tf_op jit(solution)/shard_map/pallas_call | solution.py:579
